TPU v7x, 256 devices: a whole 4x4x8 slice. The times are simulated.
256 devices in a mesh: space: 32 (over z_hi, x, core), tm: 8 (over z_lo, y).
Axes of the slice: x: 4, y: 4, z: 8 (z_hi: 4, z_lo: 2; z = z_hi * 2 + z_lo), core: 2. Of those that a mesh axis runs over, the one named last changes fastest.
Arguments:
- start_state: float32 [1024, 8192], P('space'), may hold values from -6 to 6
- old_starts: float32 [8, 1024, 8192], P('tm', 'space'), may hold values from -6 to 6
- conductivity: float32 [1024, 8192], P('space'), may hold values from 0.1 to 0.7
- velocity: float32 [2, 1024, 8192], P(None, 'space'), may hold values from -0.2 to 0.2
- coarse_gain: float32 [8, 1024, 8192], P('tm', 'space'), may hold values from 0.4 to 0.99
- targets: float32 [8, 1024, 8192], P('tm', 'space'), may hold values from -6 to 6
Outputs:
- new_ends: float32 [8, 1024, 8192], P('tm', 'space')
- gradient: float32 [1024, 8192], P('space')
All inputs are finite; a program needn't handle non-finite values.
Results may differ from a plain program's by a relative error of at most 0.00002.
Values sent between devices are 32-bit elements; how exact they have to be, the bound alone decides.
A program may use at most 128 MiB of HBM per device.

v0:
```python
import jax
import jax.numpy as jnp
from jax import lax
from jax.sharding import PartitionSpec as P

STEPS = 4
HALO = 8
time_step = 0.25


def with_halo(cells, axis, dim):
    count = lax.axis_size(axis)
    ends = count - 1
    head = lax.slice_in_dim(cells, 0, 1, axis=dim)
    tail = lax.slice_in_dim(cells, cells.shape[dim] - 1, cells.shape[dim], axis=dim)
    return jnp.concatenate(
        [
            lax.ppermute(tail, axis, [(i, (i + 1) % count) for i in range(ends)]),
            cells,
            lax.ppermute(head, axis, [((i + 1) % count, i) for i in range(ends)]),
        ],
        axis=dim,
    )


def potential(field):
    return field + 0.25 * jnp.tanh(field)


def advance(padded, kappa, along_rows, along_cols):
    wide = jnp.pad(padded, ((0, 0), (0, 0), (1, 1)))
    shaped = potential(wide)
    centre = wide[:, 1:-1, 1:-1]
    spread = (
        shaped[:, :-2, 1:-1]
        + shaped[:, 2:, 1:-1]
        + shaped[:, 1:-1, :-2]
        + shaped[:, 1:-1, 2:]
        - 4.0 * shaped[:, 1:-1, 1:-1]
    )
    transport = (
        jnp.maximum(along_rows, 0.0) * (centre - wide[:, :-2, 1:-1])
        + jnp.minimum(along_rows, 0.0) * (wide[:, 2:, 1:-1] - centre)
        + jnp.maximum(along_cols, 0.0) * (centre - wide[:, 1:-1, :-2])
        + jnp.minimum(along_cols, 0.0) * (wide[:, 1:-1, 2:] - centre)
    )
    return centre + time_step * (kappa * spread - transport)


def fine(field, kappa, along_rows, along_cols, inside):
    for step in range(STEPS):
        padded = with_halo(field, "space", 1)
        field = jnp.where(inside, advance(padded, kappa, along_rows, along_cols), 0.0)
    return field


def pad_cols(x):
    return jnp.pad(x, [(0, 0)] * (x.ndim - 1) + [(HALO, HALO)])


def own_window(x, start, width):
    return lax.dynamic_slice_in_dim(pad_cols(x), start, width, axis=x.ndim - 1)


def on_device(start_state, old_starts, conductivity, velocity, coarse_gain, targets):
    blocks = lax.axis_size("tm")
    block = lax.axis_index("tm")
    rows, cols = start_state.shape
    width = cols // blocks
    wide = width + 2 * HALO

    def send_windows(x):
        padded = pad_cols(x)
        return jnp.stack([padded[:, k * width : k * width + wide] for k in range(blocks)])

    def to_blocks(x):
        return lax.all_to_all(send_windows(x), "tm", 0, 0, tiled=True)

    old = to_blocks(old_starts[0])
    gain = to_blocks(coarse_gain[0])
    target = to_blocks(targets[0])
    first = block * width
    kappa = own_window(conductivity, first, wide)
    flow = own_window(velocity, first, wide)
    begin = own_window(start_state, first, wide)
    column = first - HALO + lax.broadcasted_iota(jnp.int32, (1, 1, wide), 2)
    inside = (column >= 0) & (column < cols)
    fine_ends, pullback = jax.vjp(lambda k: fine(old, k, flow[0], flow[1], inside), kappa)
    carried = fine_ends - gain * old
    ends = []
    for slab in range(blocks):
        begin = gain[slab] * begin + carried[slab]
        ends.append(begin)
    new_ends = jnp.stack(ends)
    misfit = new_ends - target
    adjoints = [misfit[blocks - 1]]
    for slab in range(blocks - 2, -1, -1):
        adjoints.insert(0, misfit[slab] + gain[slab + 1] * adjoints[0])
    adjoint = jnp.stack(adjoints)
    (grad_window,) = pullback(adjoint)
    interior = new_ends[:, :, HALO : HALO + width]
    new_end = lax.all_to_all(interior, "tm", 0, 2, tiled=True)
    gradient = lax.all_gather(grad_window[:, HALO : HALO + width], "tm", axis=1, tiled=True)
    return (new_end, gradient)


def solution(mesh):
    in_specs = (
        P("space", None),
        P("tm", "space", None),
        P("space", None),
        P(None, "space", None),
        P("tm", "space", None),
        P("tm", "space", None),
    )
    out_specs = (P("tm", "space", None), P("space", None))
    return jax.shard_map(
        on_device, mesh=mesh, in_specs=in_specs, out_specs=out_specs, check_vma=False
    )
```

profile of v0, /device:TPU:2, one launch (start us, length us, event | category | flops | bytes accessed | tf_op | source)
XLA Modules:
  0.0 241.2 jit_solution(3339310915675040073)
XLA Ops:
  14.3 6.0 %all-to-all-start.1 = ((f32[8,32,1040]{2,1,0:T(8,128)}), f32[8,32,1040]{2,1,0:T(8,128)S(1)}, u32[]{:S(2)}, u32[]{:S(2)}) async-start(f32[8,32,1040]{2,1,0:T(8,128)} %fusion.80), calls=%async_computation.1 | async-start | bytes 2359296 | tf_op jit(solution)/shard_map/all_to_all | solution.py:77
  32.8 3.6 %all-to-all-done.1 = f32[8,32,1040]{2,1,0:T(8,128)S(1)} async-done(((f32[8,32,1040]{2,1,0:T(8,128)}), f32[8,32,1040]{2,1,0:T(8,128)S(1)}, u32[]{:S(2)}, u32[]{:S(2)}) %all-to-all-start.1) | async-done | bytes 1064992 | tf_op jit(solution)/shard_map/all_to_all | solution.py:77
  36.5 3.6 %all-to-all-start = ((f32[8,32,1040]{2,1,0:T(8,128)}), f32[8,32,1040]{2,1,0:T(8,128)S(1)}, u32[]{:S(2)}, u32[]{:S(2)}) async-start(f32[8,32,1040]{2,1,0:T(8,128)} %fusion.76), calls=%async_computation | async-start | bytes 2359296 | tf_op jit(solution)/shard_map/all_to_all | solution.py:77
  40.1 1.9 collective-permute-start
  42.1 3.6 %collective-permute-start.1 = (f32[8,1,1040]{2,1,0:T(1,128)S(1)}, f32[8,1,1040]{2,1,0:T(1,128)S(1)}, u32[]{:S(2)}, u32[]{:S(2)}) collective-permute-start(f32[8,1,1040]{2,1,0:T(1,128)S(1)} %get-tuple-element.76), channel_id=1, source_target_pairs={{8,0},{16,8},{24,16},{32,24},{40,32},{48,40},{56,48},{64,56},{72,6... | collective-permute-start | bytes 99848 | tf_op jit(solution)/shard_map/jvp()/ppermute | solution.py:20
  48.0 3.0 %fusion.58 = (f32[8,32,1040]{2,1,0:T(8,128)S(1)}, f32[8,32,1040]{2,1,0:T(8,128)}) fusion(f32[8,32,1040]{2,1,0:T(8,128)S(1)} %all-to-all-done.1, f32[8,34,1042]{2,1,0:T(8,128)S(1)} %get-tuple-element.66, f32[8,1,1040]{2,1,0:T(1,128)S(1)} %collective-permute-done.1, f32[8,1,1040]{2,1,0:T(1,128)S(1)} %collective-permute-done, ...), kind=kLoop, calls=%fused_computation.105 | loop fusion | flops 6123520 | bytes 11382800 | tf_op jit(solution)/shard_map/jvp(jit(_where))/select_n | solution.py:53
  51.1 3.8 %collective-permute-start.2 = (f32[8,1,1040]{2,1,0:T(1,128)S(1)}, f32[8,1,1040]{2,1,0:T(1,128)S(1)}, u32[]{:S(2)}, u32[]{:S(2)}) collective-permute-start(f32[8,1,1040]{2,1,0:T(1,128)S(1)} %get-tuple-element.73), channel_id=1, source_target_pairs={{0,8},{8,16},{16,24},{24,32},{32,40},{40,48},{48,56},{56,64},{64,7... | collective-permute-start | bytes 99848 | tf_op jit(solution)/shard_map/jvp()/ppermute | solution.py:18
  54.9 2.1 collective-permute-start.3
  59.3 3.0 %fusion.44 = (f32[8,32,1040]{2,1,0:T(8,128)S(1)}, f32[8,32,1040]{2,1,0:T(8,128)}) fusion(f32[8,32,1040]{2,1,0:T(8,128)S(1)} %get-tuple-element.32, f32[8,34,1042]{2,1,0:T(8,128)S(1)} %get-tuple-element.64, f32[8,1,1040]{2,1,0:T(1,128)S(1)} %collective-permute-done.3, f32[8,1,1040]{2,1,0:T(1,128)S(1)} %collective-permute-done.2, ...), kind=kLoop, calls=%fused_computation.83 | loop fusion | flops 6123520 | bytes 11382800 | tf_op jit(solution)/shard_map/jvp(jit(_where))/select_n | solution.py:53
  62.3 3.5 %collective-permute-start.4 = (f32[8,1,1040]{2,1,0:T(1,128)S(1)}, f32[8,1,1040]{2,1,0:T(1,128)S(1)}, u32[]{:S(2)}, u32[]{:S(2)}) collective-permute-start(f32[8,1,1040]{2,1,0:T(1,128)S(1)} %get-tuple-element.71), channel_id=1, source_target_pairs={{0,8},{8,16},{16,24},{24,32},{32,40},{40,48},{48,56},{56,64},{64,7... | collective-permute-start | bytes 99848 | tf_op jit(solution)/shard_map/jvp()/ppermute | solution.py:18
  65.8 2.1 collective-permute-start.5
  70.2 3.0 %fusion.30 = (f32[8,32,1040]{2,1,0:T(8,128)S(1)}, f32[8,32,1040]{2,1,0:T(8,128)}) fusion(f32[8,32,1040]{2,1,0:T(8,128)S(1)} %get-tuple-element.30, f32[8,34,1042]{2,1,0:T(8,128)S(1)} %get-tuple-element.62, f32[8,1,1040]{2,1,0:T(1,128)S(1)} %collective-permute-done.5, f32[8,1,1040]{2,1,0:T(1,128)S(1)} %collective-permute-done.4, ...), kind=kLoop, calls=%fused_computation.61 | loop fusion | flops 6123520 | bytes 11382800 | tf_op jit(solution)/shard_map/jvp(jit(_where))/select_n | solution.py:53
  73.3 7.5 %collective-permute-start.6 = (f32[8,1,1040]{2,1,0:T(1,128)S(1)}, f32[8,1,1040]{2,1,0:T(1,128)S(1)}, u32[]{:S(2)}, u32[]{:S(2)}) collective-permute-start(f32[8,1,1040]{2,1,0:T(1,128)S(1)} %get-tuple-element.69), channel_id=1, source_target_pairs={{0,8},{8,16},{16,24},{24,32},{32,40},{40,48},{48,56},{56,64},{64,7... | collective-permute-start | bytes 99848 | tf_op jit(solution)/shard_map/jvp()/ppermute | solution.py:18
  80.7 1.9 collective-permute-start.7
  83.4 2.9 %collective-permute-done.7 = f32[8,1,1040]{2,1,0:T(1,128)S(1)} collective-permute-done((f32[8,1,1040]{2,1,0:T(1,128)S(1)}, f32[8,1,1040]{2,1,0:T(1,128)S(1)}, u32[]{:S(2)}, u32[]{:S(2)}) %collective-permute-start.7) | collective-permute-done | bytes 33312 | tf_op jit(solution)/shard_map/jvp()/ppermute | solution.py:20
  88.7 7.3 %all-to-all-start.3 = ((f32[8,32,1040]{2,1,0:T(8,128)}), f32[8,32,1040]{2,1,0:T(8,128)}, u32[]{:S(2)}, u32[]{:S(2)}) async-start(f32[8,32,1040]{2,1,0:T(8,128)} %fusion.84), calls=%async_computation.3 | async-start | bytes 2359296 | tf_op jit(solution)/shard_map/all_to_all | solution.py:77
  96.0 6.1 %fusion.16 = (f32[8,32,1040]{2,1,0:T(8,128)S(1)}, f32[8,32,1040]{2,1,0:T(8,128)}) fusion(f32[8,32,1040]{2,1,0:T(8,128)} %copy-done.4, f32[8,34,1042]{2,1,0:T(8,128)} %get-tuple-element.60, f32[8,1,1040]{2,1,0:T(1,128)} %copy-done.32, f32[8,1,1040]{2,1,0:T(1,128)} %copy-done.30, f32[8,32,1040]{2,1,0:T(8,128)S(1)} %all-to-all-done, ...), kind=kLoop, calls=%fused_computation.39 | loop fusion | flops 6656000 | bytes 13512720 | tf_op jit(solution)/shard_map/sub | solution.py:89
  102.5 6.3 %all-to-all-done.3 = f32[8,32,1040]{2,1,0:T(8,128)} async-done(((f32[8,32,1040]{2,1,0:T(8,128)}), f32[8,32,1040]{2,1,0:T(8,128)}, u32[]{:S(2)}, u32[]{:S(2)}) %all-to-all-start.3) | async-done | bytes 1064992 | tf_op jit(solution)/shard_map/all_to_all | solution.py:77
  112.2 4.6 %multiply_add_fusion.2 = f32[8,34,1042]{2,1,0:T(8,128)S(1)} fusion(f32[8,32,1040]{2,1,0:T(8,128)S(1)} %get-tuple-element.68, f32[8,32,1040]{2,1,0:T(8,128)S(1)} %get-tuple-element.67, f32[8,32,1040]{2,1,0:T(8,128)S(1)} %get-tuple-element.55, f32[8,32,1040]{2,1,0:T(8,128)S(1)} %get-tuple-element.56, f32[8,32,1040]{2,1,0:T(8,128)S(1)} %get-tuple-element.57, ...), kind=kLoop, calls=%fused_computation.14 | loop fusion | flops 6518752 | bytes 9719936 | tf_op jit(solution)/shard_map/transpose(jvp())/add_any | solution.py:27
  117.1 1.9 collective-permute-start.8
  119.0 6.7 %collective-permute-start.9 = (f32[8,1,1040]{2,1,0:T(1,128)S(1)}, f32[8,1,1040]{2,1,0:T(1,128)S(1)}, u32[]{:S(2)}, u32[]{:S(2)}) collective-permute-start(f32[8,1,1040]{2,1,0:T(1,128)S(1)} %get-tuple-element.53), channel_id=1, source_target_pairs={{0,8},{8,16},{16,24},{24,32},{32,40},{40,48},{48,56},{56,64},{64,7... | collective-permute-start | bytes 99848 | tf_op jit(solution)/shard_map/transpose(jvp())/ppermute | solution.py:20
  128.4 4.6 %multiply_add_fusion.1 = f32[8,34,1042]{2,1,0:T(8,128)S(1)} fusion(f32[8,32,1040]{2,1,0:T(8,128)S(1)} %get-tuple-element.9, f32[8,32,1040]{2,1,0:T(8,128)S(1)} %get-tuple-element.8, f32[8,32,1040]{2,1,0:T(8,128)S(1)} %get-tuple-element.43, f32[8,32,1040]{2,1,0:T(8,128)S(1)} %get-tuple-element.44, f32[8,32,1040]{2,1,0:T(8,128)S(1)} %get-tuple-element.45, ...), kind=kLoop, calls=%fused_computation.13 | loop fusion | flops 6518752 | bytes 9719936 | tf_op jit(solution)/shard_map/transpose(jvp())/add_any | solution.py:27
  133.2 1.9 collective-permute-start.10
  135.2 4.1 %collective-permute-start.11 = (f32[8,1,1040]{2,1,0:T(1,128)S(1)}, f32[8,1,1040]{2,1,0:T(1,128)S(1)}, u32[]{:S(2)}, u32[]{:S(2)}) collective-permute-start(f32[8,1,1040]{2,1,0:T(1,128)S(1)} %get-tuple-element.51), channel_id=1, source_target_pairs={{0,8},{8,16},{16,24},{24,32},{32,40},{40,48},{48,56},{56,64},{64,7... | collective-permute-start | bytes 99848 | tf_op jit(solution)/shard_map/transpose(jvp())/ppermute | solution.py:20
  142.3 4.6 %multiply_add_fusion = f32[8,34,1042]{2,1,0:T(8,128)S(1)} fusion(f32[8,32,1040]{2,1,0:T(8,128)S(1)} %get-tuple-element.7, f32[8,32,1040]{2,1,0:T(8,128)S(1)} %get-tuple-element.6, f32[8,32,1040]{2,1,0:T(8,128)S(1)} %get-tuple-element.39, f32[8,32,1040]{2,1,0:T(8,128)S(1)} %get-tuple-element.40, f32[8,32,1040]{2,1,0:T(8,128)S(1)} %get-tuple-element.41, ...), kind=kLoop, calls=%fused_computation.12 | loop fusion | flops 6518752 | bytes 9719936 | tf_op jit(solution)/shard_map/transpose(jvp())/add_any | solution.py:27
  150.3 4.5 %collective-permute-start.13 = (f32[8,1,1040]{2,1,0:T(1,128)S(1)}, f32[8,1,1040]{2,1,0:T(1,128)S(1)}, u32[]{:S(2)}, u32[]{:S(2)}) collective-permute-start(f32[8,1,1040]{2,1,0:T(1,128)S(1)} %get-tuple-element.49), channel_id=1, source_target_pairs={{0,8},{8,16},{16,24},{24,32},{32,40},{40,48},{48,56},{56,64},{64,7... | collective-permute-start | bytes 99848 | tf_op jit(solution)/shard_map/transpose(jvp())/ppermute | solution.py:20
  156.1 5.8 %all-to-all-start.2 = ((f32[8,32,1024]{2,1,0:T(8,128)}), f32[8,32,1024]{2,1,0:T(8,128)}, u32[]{:S(2)}, u32[]{:S(2)}) async-start(f32[8,32,1024]{2,1,0:T(8,128)} %slice.509), calls=%async_computation.2 | async-start | bytes 2097152 | tf_op jit(solution)/shard_map/all_to_all | solution.py:102
  162.5 4.6 %multiply_reduce_fusion.2 = (f32[32,1040]{1,0:T(8,128)S(1)}, f32[32,1040]{1,0:T(8,128)S(1)}, f32[32,1040]{1,0:T(8,128)S(1)}, f32[32,1040]{1,0:T(8,128)S(1)}) fusion(f32[8,32,1040]{2,1,0:T(8,128)} %get-tuple-element.27, f32[8,32,1040]{2,1,0:T(8,128)} %copy-done.11, pred[1040]{0:T(1024)(128)(4,1)S(1)} %fusion.117, f32[8,32,1040]{2,1,0:T(8,128)} %get-tuple-element.29, ...), kind=kLoop, calls=%fused_computation.129 | loop fusion | flops 5724160 | bytes 9252880 | tf_op jit(solution)/shard_map/transpose(jvp())/reduce_sum | solution.py:47
  168.0 9.7 %all-to-all-done.2 = f32[8,32,1024]{2,1,0:T(8,128)} async-done(((f32[8,32,1024]{2,1,0:T(8,128)}), f32[8,32,1024]{2,1,0:T(8,128)}, u32[]{:S(2)}, u32[]{:S(2)}) %all-to-all-start.2) | async-done | bytes 1048608 | tf_op jit(solution)/shard_map/all_to_all | solution.py:102
  177.8 2.3 copy.9
  180.1 52.0 %all-gather.2.cloned.1.call-done = f32[32,8192]{1,0:T(8,128)} async-done(((f32[32,1024]{1,0:T(8,128)}), f32[32,8192]{1,0:T(8,128)}) %all-gather.2.cloned.1.call-update) | async-done | bytes 1048592 | tf_op jit(solution)/shard_map/all_gather | solution.py:103
  232.1 2.3 copy.46
  (151 shorter events, 45.9 us)
Async XLA Ops:
  7.2 1.8 copy-start.7
  14.3 6.0 %copy-start.8 = (f32[1,32,8192]{2,1,0:T(8,128)S(1)}, f32[1,32,8192]{2,1,0:T(8,128)}, u32[]{:S(2)}) copy-start(f32[1,32,8192]{2,1,0:T(8,128)} %param.10) | copy-start | bytes 3145732
  14.3 22.2 %all-to-all-start.1 = ((f32[8,32,1040]{2,1,0:T(8,128)}), f32[8,32,1040]{2,1,0:T(8,128)S(1)}, u32[]{:S(2)}, u32[]{:S(2)}) async-start(f32[8,32,1040]{2,1,0:T(8,128)} %fusion.80), calls=%async_computation.1 | async-start | bytes 2359296 | tf_op jit(solution)/shard_map/all_to_all | solution.py:77
  27.4 99.1 %copy-start.15 = (f32[32,1040]{1,0:T(8,128)}, f32[32,1040]{1,0:T(8,128)S(1)}, u32[]{:S(2)}) copy-start(f32[32,1040]{1,0:T(8,128)S(1)} %get-tuple-element.12) | copy-start | bytes 399364
  36.5 11.5 %copy-start.6 = (f32[8,32,1040]{2,1,0:T(8,128)}, f32[8,32,1040]{2,1,0:T(8,128)S(1)}, u32[]{:S(2)}) copy-start(f32[8,32,1040]{2,1,0:T(8,128)S(1)} %all-to-all-done.1) | copy-start | bytes 3194884
  36.5 52.3 %all-to-all-start = ((f32[8,32,1040]{2,1,0:T(8,128)}), f32[8,32,1040]{2,1,0:T(8,128)S(1)}, u32[]{:S(2)}, u32[]{:S(2)}) async-start(f32[8,32,1040]{2,1,0:T(8,128)} %fusion.76), calls=%async_computation | async-start | bytes 2359296 | tf_op jit(solution)/shard_map/all_to_all | solution.py:77
  40.1 5.6 %collective-permute-start = (f32[8,1,1040]{2,1,0:T(1,128)S(1)}, f32[8,1,1040]{2,1,0:T(1,128)S(1)}, u32[]{:S(2)}, u32[]{:S(2)}) collective-permute-start(f32[8,1,1040]{2,1,0:T(1,128)S(1)} %get-tuple-element.75), channel_id=1, source_target_pairs={{0,8},{8,16},{16,24},{24,32},{32,40},{40,48},{48,56},{56,64},{64,7... | collective-permute-start | bytes 99848 | tf_op jit(solution)/shard_map/jvp()/ppermute | solution.py:18
  42.1 5.3 %collective-permute-start.1 = (f32[8,1,1040]{2,1,0:T(1,128)S(1)}, f32[8,1,1040]{2,1,0:T(1,128)S(1)}, u32[]{:S(2)}, u32[]{:S(2)}) collective-permute-start(f32[8,1,1040]{2,1,0:T(1,128)S(1)} %get-tuple-element.76), channel_id=1, source_target_pairs={{8,0},{16,8},{24,16},{32,24},{40,32},{48,40},{56,48},{64,56},{72,6... | collective-permute-start | bytes 99848 | tf_op jit(solution)/shard_map/jvp()/ppermute | solution.py:20
  48.0 9.0 %copy-start.10 = (f32[1,32,8192]{2,1,0:T(8,128)S(1)}, f32[1,32,8192]{2,1,0:T(8,128)}, u32[]{:S(2)}) copy-start(f32[1,32,8192]{2,1,0:T(8,128)} %param.11) | copy-start | bytes 3145732
  51.0 8.2 %copy-start = (f32[8,32,1040]{2,1,0:T(8,128)}, f32[8,32,1040]{2,1,0:T(8,128)S(1)}, u32[]{:S(2)}) copy-start(f32[8,32,1040]{2,1,0:T(8,128)S(1)} %get-tuple-element.32) | copy-start | bytes 3194884
  51.1 6.7 %collective-permute-start.2 = (f32[8,1,1040]{2,1,0:T(1,128)S(1)}, f32[8,1,1040]{2,1,0:T(1,128)S(1)}, u32[]{:S(2)}, u32[]{:S(2)}) collective-permute-start(f32[8,1,1040]{2,1,0:T(1,128)S(1)} %get-tuple-element.73), channel_id=1, source_target_pairs={{0,8},{8,16},{16,24},{24,32},{32,40},{40,48},{48,56},{56,64},{64,7... | collective-permute-start | bytes 99848 | tf_op jit(solution)/shard_map/jvp()/ppermute | solution.py:18
  54.9 3.7 %collective-permute-start.3 = (f32[8,1,1040]{2,1,0:T(1,128)S(1)}, f32[8,1,1040]{2,1,0:T(1,128)S(1)}, u32[]{:S(2)}, u32[]{:S(2)}) collective-permute-start(f32[8,1,1040]{2,1,0:T(1,128)S(1)} %get-tuple-element.74), channel_id=1, source_target_pairs={{8,0},{16,8},{24,16},{32,24},{40,32},{48,40},{56,48},{64,56},{72,6... | collective-permute-start | bytes 99848 | tf_op jit(solution)/shard_map/jvp()/ppermute | solution.py:20
  62.3 7.9 %copy-start.2 = (f32[8,32,1040]{2,1,0:T(8,128)}, f32[8,32,1040]{2,1,0:T(8,128)S(1)}, u32[]{:S(2)}) copy-start(f32[8,32,1040]{2,1,0:T(8,128)S(1)} %get-tuple-element.30) | copy-start | bytes 3194884
  62.3 6.4 %collective-permute-start.4 = (f32[8,1,1040]{2,1,0:T(1,128)S(1)}, f32[8,1,1040]{2,1,0:T(1,128)S(1)}, u32[]{:S(2)}, u32[]{:S(2)}) collective-permute-start(f32[8,1,1040]{2,1,0:T(1,128)S(1)} %get-tuple-element.71), channel_id=1, source_target_pairs={{0,8},{8,16},{16,24},{24,32},{32,40},{40,48},{48,56},{56,64},{64,7... | collective-permute-start | bytes 99848 | tf_op jit(solution)/shard_map/jvp()/ppermute | solution.py:18
  65.8 3.7 %collective-permute-start.5 = (f32[8,1,1040]{2,1,0:T(1,128)S(1)}, f32[8,1,1040]{2,1,0:T(1,128)S(1)}, u32[]{:S(2)}, u32[]{:S(2)}) collective-permute-start(f32[8,1,1040]{2,1,0:T(1,128)S(1)} %get-tuple-element.72), channel_id=1, source_target_pairs={{8,0},{16,8},{24,16},{32,24},{40,32},{48,40},{56,48},{64,56},{72,6... | collective-permute-start | bytes 99848 | tf_op jit(solution)/shard_map/jvp()/ppermute | solution.py:20
  73.2 13.1 %copy-start.4 = (f32[8,32,1040]{2,1,0:T(8,128)}, f32[8,32,1040]{2,1,0:T(8,128)S(1)}, u32[]{:S(2)}) copy-start(f32[8,32,1040]{2,1,0:T(8,128)S(1)} %get-tuple-element.28) | copy-start | bytes 3194884
  73.3 10.2 %collective-permute-start.6 = (f32[8,1,1040]{2,1,0:T(1,128)S(1)}, f32[8,1,1040]{2,1,0:T(1,128)S(1)}, u32[]{:S(2)}, u32[]{:S(2)}) collective-permute-start(f32[8,1,1040]{2,1,0:T(1,128)S(1)} %get-tuple-element.69), channel_id=1, source_target_pairs={{0,8},{8,16},{16,24},{24,32},{32,40},{40,48},{48,56},{56,64},{64,7... | collective-permute-start | bytes 99848 | tf_op jit(solution)/shard_map/jvp()/ppermute | solution.py:18
  80.7 5.6 %collective-permute-start.7 = (f32[8,1,1040]{2,1,0:T(1,128)S(1)}, f32[8,1,1040]{2,1,0:T(1,128)S(1)}, u32[]{:S(2)}, u32[]{:S(2)}) collective-permute-start(f32[8,1,1040]{2,1,0:T(1,128)S(1)} %get-tuple-element.70), channel_id=1, source_target_pairs={{8,0},{16,8},{24,16},{32,24},{40,32},{48,40},{56,48},{64,56},{72,6... | collective-permute-start | bytes 99848 | tf_op jit(solution)/shard_map/jvp()/ppermute | solution.py:20
  83.4 2.9 %copy-start.30 = (f32[8,1,1040]{2,1,0:T(1,128)}, f32[8,1,1040]{2,1,0:T(1,128)S(1)}, u32[]{:S(2)}) copy-start(f32[8,1,1040]{2,1,0:T(1,128)S(1)} %collective-permute-done.6) | copy-start | bytes 99844
  88.7 20.0 %all-to-all-start.3 = ((f32[8,32,1040]{2,1,0:T(8,128)}), f32[8,32,1040]{2,1,0:T(8,128)}, u32[]{:S(2)}, u32[]{:S(2)}) async-start(f32[8,32,1040]{2,1,0:T(8,128)} %fusion.84), calls=%async_computation.3 | async-start | bytes 2359296 | tf_op jit(solution)/shard_map/all_to_all | solution.py:77
  96.0 6.1 %copy-start.17 = (f32[32,8192]{1,0:T(8,128)S(1)}, f32[32,8192]{1,0:T(8,128)}, u32[]{:S(2)}) copy-start(f32[32,8192]{1,0:T(8,128)} %param.6) | copy-start | bytes 3145732
  102.5 7.7 %copy-start.13 = (f32[8,32,1040]{2,1,0:T(8,128)}, f32[8,32,1040]{2,1,0:T(8,128)S(1)}, u32[]{:S(2)}) copy-start(f32[8,32,1040]{2,1,0:T(8,128)S(1)} %fusion.96) | copy-start | bytes 3194884
  117.1 8.6 %collective-permute-start.8 = (f32[8,1,1040]{2,1,0:T(1,128)S(1)}, f32[8,1,1040]{2,1,0:T(1,128)S(1)}, u32[]{:S(2)}, u32[]{:S(2)}) collective-permute-start(f32[8,1,1040]{2,1,0:T(1,128)S(1)} %get-tuple-element.52), channel_id=1, source_target_pairs={{8,0},{16,8},{24,16},{32,24},{40,32},{48,40},{56,48},{64,56},{72,6... | collective-permute-start | bytes 99848 | tf_op jit(solution)/shard_map/transpose(jvp())/ppermute | solution.py:18
  119.0 7.5 %collective-permute-start.9 = (f32[8,1,1040]{2,1,0:T(1,128)S(1)}, f32[8,1,1040]{2,1,0:T(1,128)S(1)}, u32[]{:S(2)}, u32[]{:S(2)}) collective-permute-start(f32[8,1,1040]{2,1,0:T(1,128)S(1)} %get-tuple-element.53), channel_id=1, source_target_pairs={{0,8},{8,16},{16,24},{24,32},{32,40},{40,48},{48,56},{56,64},{64,7... | collective-permute-start | bytes 99848 | tf_op jit(solution)/shard_map/transpose(jvp())/ppermute | solution.py:20
  128.4 12.0 %copy-start.16 = (f32[32,1040]{1,0:T(8,128)S(1)}, f32[32,1040]{1,0:T(8,128)}, u32[]{:S(2)}) copy-start(f32[32,1040]{1,0:T(8,128)} %copy-done.15) | copy-start | bytes 399364
  133.2 6.0 %collective-permute-start.10 = (f32[8,1,1040]{2,1,0:T(1,128)S(1)}, f32[8,1,1040]{2,1,0:T(1,128)S(1)}, u32[]{:S(2)}, u32[]{:S(2)}) collective-permute-start(f32[8,1,1040]{2,1,0:T(1,128)S(1)} %get-tuple-element.50), channel_id=1, source_target_pairs={{8,0},{16,8},{24,16},{32,24},{40,32},{48,40},{56,48},{64,56},{72,6... | collective-permute-start | bytes 99848 | tf_op jit(solution)/shard_map/transpose(jvp())/ppermute | solution.py:18
  135.2 5.3 %collective-permute-start.11 = (f32[8,1,1040]{2,1,0:T(1,128)S(1)}, f32[8,1,1040]{2,1,0:T(1,128)S(1)}, u32[]{:S(2)}, u32[]{:S(2)}) collective-permute-start(f32[8,1,1040]{2,1,0:T(1,128)S(1)} %get-tuple-element.51), channel_id=1, source_target_pairs={{0,8},{8,16},{16,24},{24,32},{32,40},{40,48},{48,56},{56,64},{64,7... | collective-permute-start | bytes 99848 | tf_op jit(solution)/shard_map/transpose(jvp())/ppermute | solution.py:20
  142.3 12.4 %copy-start.14 = (f32[8,32,1040]{2,1,0:T(8,128)S(1)}, f32[8,32,1040]{2,1,0:T(8,128)}, u32[]{:S(2)}) copy-start(f32[8,32,1040]{2,1,0:T(8,128)} %copy-done.13) | copy-start | bytes 3194884
  148.3 13.6 %collective-permute-start.12 = (f32[8,1,1040]{2,1,0:T(1,128)S(1)}, f32[8,1,1040]{2,1,0:T(1,128)S(1)}, u32[]{:S(2)}, u32[]{:S(2)}) collective-permute-start(f32[8,1,1040]{2,1,0:T(1,128)S(1)} %get-tuple-element.48), channel_id=1, source_target_pairs={{8,0},{16,8},{24,16},{32,24},{40,32},{48,40},{56,48},{64,56},{72,6... | collective-permute-start | bytes 99848 | tf_op jit(solution)/shard_map/transpose(jvp())/ppermute | solution.py:18
  150.3 11.7 %collective-permute-start.13 = (f32[8,1,1040]{2,1,0:T(1,128)S(1)}, f32[8,1,1040]{2,1,0:T(1,128)S(1)}, u32[]{:S(2)}, u32[]{:S(2)}) collective-permute-start(f32[8,1,1040]{2,1,0:T(1,128)S(1)} %get-tuple-element.49), channel_id=1, source_target_pairs={{0,8},{8,16},{16,24},{24,32},{32,40},{40,48},{48,56},{56,64},{64,7... | collective-permute-start | bytes 99848 | tf_op jit(solution)/shard_map/transpose(jvp())/ppermute | solution.py:20
  156.1 21.7 %all-to-all-start.2 = ((f32[8,32,1024]{2,1,0:T(8,128)}), f32[8,32,1024]{2,1,0:T(8,128)}, u32[]{:S(2)}, u32[]{:S(2)}) async-start(f32[8,32,1024]{2,1,0:T(8,128)} %slice.509), calls=%async_computation.2 | async-start | bytes 2097152 | tf_op jit(solution)/shard_map/all_to_all | solution.py:102
  161.9 70.3 %all-gather.2.cloned.1.call-start = ((), (), s32[]{:S(2)}) async-start(), calls=%async_computation.4 | async-start | bytes 1179648 | tf_op jit(solution)/shard_map/all_gather | solution.py:103
  (23 other events, 27.2 us)
Sparse Core Ops, SparseCore 0:
  168.2 63.9 all-gather.1
where the time goes:
time: 242 us; the launch traced here: 241 us
  waiting for transfers between devices  79.9 us (33%)
  starting transfers between devices  70 us (29%)
  other arithmetic  46.4 us (19%)
  local copies, waits for them, and re-layouts  30.3 us (13%)
  between operations  14.6 us (6%)
    all_gather x1, waiting for transfers between devices, on_device(): lax.all_gather(grad_window[:, HALO:HALO + width], 'tm', axis=1, tiled=True)  52 us
    ppermute x7, starting transfers between devices, with_halo(): lax.ppermute(head, axis, [((i + 1) % count, i) for i in range(ends)])  24.9 us
    unnamed x97, local copies, waits for them, and re-layouts  23.5 us
    ppermute x7, starting transfers between devices, with_halo(): lax.ppermute(tail, axis, [(i, (i + 1) % count) for i in range(ends)])  22.5 us
    all_to_all x3, starting transfers between devices, to_blocks(): return lax.all_to_all(send_windows(x), 'tm', 0, 0, tiled=True)  16.8 us
    add_any x3, other arithmetic, potential(): return field + 0.25 * jnp.tanh(field)  13.8 us
    all_to_all x3, waiting for transfers between devices, to_blocks(): return lax.all_to_all(send_windows(x), 'tm', 0, 0, tiled=True)  9.89 us
    all_to_all x1, waiting for transfers between devices, on_device(): new_end = lax.all_to_all(interior, 'tm', 0, 2, tiled=True)  9.73 us
  transfers between devices with their start and end apart: 19, of which 10 were waited for; matrix products, arithmetic and copies ran while one was open for 18% of the time, Pallas kernels for 0%

commit v1 on v0

--- a/solution.py
+++ b/solution.py
@@ -100,7 +100,13 @@
     (grad_window,) = pullback(adjoint)
     interior = new_ends[:, :, HALO : HALO + width]
     new_end = lax.all_to_all(interior, "tm", 0, 2, tiled=True)
-    gradient = lax.all_gather(grad_window[:, HALO : HALO + width], "tm", axis=1, tiled=True)
+    streams_order = lambda field_in, named_axis: jnp.concatenate(
+        lax.all_to_all(
+            jnp.stack([field_in for _ in range(lax.psum(1, named_axis))]), named_axis, 0, 0
+        ),
+        axis=1,
+    )
+    gradient = streams_order(grad_window[:, HALO : HALO + width], "tm")
     return (new_end, gradient)
 
 

time: 242 us -> 204 us (0.84)
  the two profiles are of different devices: /device:TPU:2 before, /device:TPU:160 now
where the time goes in v1:
time: 204 us; the launch traced here: 202 us
  starting transfers between devices  88.2 us (43%)
  other arithmetic  45.3 us (22%)
  waiting for transfers between devices  39.1 us (19%)
  local copies, waits for them, and re-layouts  28.5 us (14%)
    ppermute x7, starting transfers between devices, with_halo(): lax.ppermute(head, axis, [((i + 1) % count, i) for i in range(ends)])  37.9 us
    ppermute x7, waiting for transfers between devices, with_halo(): lax.ppermute(head, axis, [((i + 1) % count, i) for i in range(ends)])  23.9 us
    ppermute x7, starting transfers between devices, with_halo(): lax.ppermute(tail, axis, [(i, (i + 1) % count) for i in range(ends)])  23.1 us
    unnamed x98, local copies, waits for them, and re-layouts  19 us
    all_to_all x3, starting transfers between devices, to_blocks(): return lax.all_to_all(send_windows(x), 'tm', 0, 0, tiled=True)  17.2 us
    add_any x3, other arithmetic, potential(): return field + 0.25 * jnp.tanh(field)  13.8 us
    select_n x3, other arithmetic, fine(): jnp.where(inside, advance(padded, kappa, along_rows, along_cols), 0.0)  8.96 us
    all_to_all x1, waiting for transfers between devices, on_device(): lax.all_to_all(jnp.stack([field_in for _ in range(lax.psum(1, named_axis)...  7.73 us
  transfers between devices with their start and end apart: 19, of which 10 were waited for; matrix products, arithmetic and copies ran while one was open for 24% of the time, Pallas kernels for 0%

profile of v1, /device:TPU:160, one launch (start us, length us, event | category | flops | bytes accessed | tf_op | source)
XLA Modules:
  0.0 202.4 jit_solution(6618003697688310424)
XLA Ops:
  7.8 6.1 %all-to-all-start.1 = ((f32[8,32,1040]{2,1,0:T(8,128)}), f32[8,32,1040]{2,1,0:T(8,128)S(1)}, u32[]{:S(2)}, u32[]{:S(2)}) async-start(f32[8,32,1040]{2,1,0:T(8,128)} %fusion.80), calls=%async_computation.1 | async-start | bytes 2359296 | tf_op jit(solution)/shard_map/all_to_all | solution.py:77
  26.4 3.1 %all-to-all-done.1 = f32[8,32,1040]{2,1,0:T(8,128)S(1)} async-done(((f32[8,32,1040]{2,1,0:T(8,128)}), f32[8,32,1040]{2,1,0:T(8,128)S(1)}, u32[]{:S(2)}, u32[]{:S(2)}) %all-to-all-start.1) | async-done | bytes 1064992 | tf_op jit(solution)/shard_map/all_to_all | solution.py:77
  29.5 4.2 %all-to-all-start = ((f32[8,32,1040]{2,1,0:T(8,128)}), f32[8,32,1040]{2,1,0:T(8,128)S(1)}, u32[]{:S(2)}, u32[]{:S(2)}) async-start(f32[8,32,1040]{2,1,0:T(8,128)} %fusion.76), calls=%async_computation | async-start | bytes 2359296 | tf_op jit(solution)/shard_map/all_to_all | solution.py:77
  33.7 1.9 collective-permute-start
  35.6 7.9 %collective-permute-start.1 = (f32[8,1,1040]{2,1,0:T(1,128)S(1)}, f32[8,1,1040]{2,1,0:T(1,128)S(1)}, u32[]{:S(2)}, u32[]{:S(2)}) collective-permute-start(f32[8,1,1040]{2,1,0:T(1,128)S(1)} %get-tuple-element.76), channel_id=1, source_target_pairs={{8,0},{16,8},{24,16},{32,24},{40,32},{48,40},{56,48},{64,56},{72,6... | collective-permute-start | bytes 99848 | tf_op jit(solution)/shard_map/jvp()/ppermute | solution.py:20
  43.5 3.7 %collective-permute-done.1 = f32[8,1,1040]{2,1,0:T(1,128)S(1)} collective-permute-done((f32[8,1,1040]{2,1,0:T(1,128)S(1)}, f32[8,1,1040]{2,1,0:T(1,128)S(1)}, u32[]{:S(2)}, u32[]{:S(2)}) %collective-permute-start.1) | collective-permute-done | bytes 33312 | tf_op jit(solution)/shard_map/jvp()/ppermute | solution.py:20
  47.9 3.0 %fusion.58 = (f32[8,32,1040]{2,1,0:T(8,128)S(1)}, f32[8,32,1040]{2,1,0:T(8,128)}) fusion(f32[8,32,1040]{2,1,0:T(8,128)S(1)} %all-to-all-done.1, f32[8,34,1042]{2,1,0:T(8,128)S(1)} %get-tuple-element.66, f32[8,1,1040]{2,1,0:T(1,128)S(1)} %collective-permute-done.1, f32[8,1,1040]{2,1,0:T(1,128)S(1)} %collective-permute-done, ...), kind=kLoop, calls=%fused_computation.105 | loop fusion | flops 6123520 | bytes 11382800 | tf_op jit(solution)/shard_map/jvp(jit(_where))/select_n | solution.py:53
  51.0 1.9 collective-permute-start.2
  52.9 8.0 %collective-permute-start.3 = (f32[8,1,1040]{2,1,0:T(1,128)S(1)}, f32[8,1,1040]{2,1,0:T(1,128)S(1)}, u32[]{:S(2)}, u32[]{:S(2)}) collective-permute-start(f32[8,1,1040]{2,1,0:T(1,128)S(1)} %get-tuple-element.74), channel_id=1, source_target_pairs={{8,0},{16,8},{24,16},{32,24},{40,32},{48,40},{56,48},{64,56},{72,6... | collective-permute-start | bytes 99848 | tf_op jit(solution)/shard_map/jvp()/ppermute | solution.py:20
  63.3 3.0 %fusion.44 = (f32[8,32,1040]{2,1,0:T(8,128)S(1)}, f32[8,32,1040]{2,1,0:T(8,128)}) fusion(f32[8,32,1040]{2,1,0:T(8,128)S(1)} %get-tuple-element.32, f32[8,34,1042]{2,1,0:T(8,128)S(1)} %get-tuple-element.64, f32[8,1,1040]{2,1,0:T(1,128)S(1)} %collective-permute-done.3, f32[8,1,1040]{2,1,0:T(1,128)S(1)} %collective-permute-done.2, ...), kind=kLoop, calls=%fused_computation.83 | loop fusion | flops 6123520 | bytes 11382800 | tf_op jit(solution)/shard_map/jvp(jit(_where))/select_n | solution.py:53
  66.3 1.9 collective-permute-start.4
  68.2 7.9 %collective-permute-start.5 = (f32[8,1,1040]{2,1,0:T(1,128)S(1)}, f32[8,1,1040]{2,1,0:T(1,128)S(1)}, u32[]{:S(2)}, u32[]{:S(2)}) collective-permute-start(f32[8,1,1040]{2,1,0:T(1,128)S(1)} %get-tuple-element.72), channel_id=1, source_target_pairs={{8,0},{16,8},{24,16},{32,24},{40,32},{48,40},{56,48},{64,56},{72,6... | collective-permute-start | bytes 99848 | tf_op jit(solution)/shard_map/jvp()/ppermute | solution.py:20
  78.4 3.0 %fusion.30 = (f32[8,32,1040]{2,1,0:T(8,128)S(1)}, f32[8,32,1040]{2,1,0:T(8,128)}) fusion(f32[8,32,1040]{2,1,0:T(8,128)S(1)} %get-tuple-element.30, f32[8,34,1042]{2,1,0:T(8,128)S(1)} %get-tuple-element.62, f32[8,1,1040]{2,1,0:T(1,128)S(1)} %collective-permute-done.5, f32[8,1,1040]{2,1,0:T(1,128)S(1)} %collective-permute-done.4, ...), kind=kLoop, calls=%fused_computation.61 | loop fusion | flops 6123520 | bytes 11382800 | tf_op jit(solution)/shard_map/jvp(jit(_where))/select_n | solution.py:53
  83.4 7.9 %collective-permute-start.7 = (f32[8,1,1040]{2,1,0:T(1,128)S(1)}, f32[8,1,1040]{2,1,0:T(1,128)S(1)}, u32[]{:S(2)}, u32[]{:S(2)}) collective-permute-start(f32[8,1,1040]{2,1,0:T(1,128)S(1)} %get-tuple-element.70), channel_id=1, source_target_pairs={{8,0},{16,8},{24,16},{32,24},{40,32},{48,40},{56,48},{64,56},{72,6... | collective-permute-start | bytes 99848 | tf_op jit(solution)/shard_map/jvp()/ppermute | solution.py:20
  95.3 7.0 %all-to-all-start.3 = ((f32[8,32,1040]{2,1,0:T(8,128)}), f32[8,32,1040]{2,1,0:T(8,128)}, u32[]{:S(2)}, u32[]{:S(2)}) async-start(f32[8,32,1040]{2,1,0:T(8,128)} %fusion.84), calls=%async_computation.3 | async-start | bytes 2359296 | tf_op jit(solution)/shard_map/all_to_all | solution.py:77
  102.3 6.0 %fusion.16 = (f32[8,32,1040]{2,1,0:T(8,128)S(1)}, f32[8,32,1040]{2,1,0:T(8,128)}) fusion(f32[8,32,1040]{2,1,0:T(8,128)} %copy-done.4, f32[8,34,1042]{2,1,0:T(8,128)} %get-tuple-element.60, f32[8,1,1040]{2,1,0:T(1,128)} %copy-done.35, f32[8,1,1040]{2,1,0:T(1,128)} %copy-done.33, f32[8,32,1040]{2,1,0:T(8,128)S(1)} %all-to-all-done, ...), kind=kLoop, calls=%fused_computation.39 | loop fusion | flops 6656000 | bytes 13512720 | tf_op jit(solution)/shard_map/sub | solution.py:89
  108.7 4.4 %all-to-all-done.3 = f32[8,32,1040]{2,1,0:T(8,128)} async-done(((f32[8,32,1040]{2,1,0:T(8,128)}), f32[8,32,1040]{2,1,0:T(8,128)}, u32[]{:S(2)}, u32[]{:S(2)}) %all-to-all-start.3) | async-done | bytes 1064992 | tf_op jit(solution)/shard_map/all_to_all | solution.py:77
  116.6 4.6 %multiply_add_fusion.2 = f32[8,34,1042]{2,1,0:T(8,128)S(1)} fusion(f32[8,32,1040]{2,1,0:T(8,128)S(1)} %get-tuple-element.68, f32[8,32,1040]{2,1,0:T(8,128)S(1)} %get-tuple-element.67, f32[8,32,1040]{2,1,0:T(8,128)S(1)} %get-tuple-element.55, f32[8,32,1040]{2,1,0:T(8,128)S(1)} %get-tuple-element.56, f32[8,32,1040]{2,1,0:T(8,128)S(1)} %get-tuple-element.57, ...), kind=kLoop, calls=%fused_computation.14 | loop fusion | flops 6518752 | bytes 9719936 | tf_op jit(solution)/shard_map/transpose(jvp())/add_any | solution.py:27
  121.4 8.0 %collective-permute-start.8 = (f32[8,1,1040]{2,1,0:T(1,128)S(1)}, f32[8,1,1040]{2,1,0:T(1,128)S(1)}, u32[]{:S(2)}, u32[]{:S(2)}) collective-permute-start(f32[8,1,1040]{2,1,0:T(1,128)S(1)} %get-tuple-element.52), channel_id=1, source_target_pairs={{8,0},{16,8},{24,16},{32,24},{40,32},{48,40},{56,48},{64,56},{72,6... | collective-permute-start | bytes 99848 | tf_op jit(solution)/shard_map/transpose(jvp())/ppermute | solution.py:18
  131.4 7.9 %collective-permute-done.9 = f32[8,1,1040]{2,1,0:T(1,128)S(1)} collective-permute-done((f32[8,1,1040]{2,1,0:T(1,128)S(1)}, f32[8,1,1040]{2,1,0:T(1,128)S(1)}, u32[]{:S(2)}, u32[]{:S(2)}) %collective-permute-start.9) | collective-permute-done | bytes 33312 | tf_op jit(solution)/shard_map/transpose(jvp())/ppermute | solution.py:20
  141.2 4.6 %multiply_add_fusion.1 = f32[8,34,1042]{2,1,0:T(8,128)S(1)} fusion(f32[8,32,1040]{2,1,0:T(8,128)S(1)} %get-tuple-element.9, f32[8,32,1040]{2,1,0:T(8,128)S(1)} %get-tuple-element.8, f32[8,32,1040]{2,1,0:T(8,128)S(1)} %get-tuple-element.43, f32[8,32,1040]{2,1,0:T(8,128)S(1)} %get-tuple-element.44, f32[8,32,1040]{2,1,0:T(8,128)S(1)} %get-tuple-element.45, ...), kind=kLoop, calls=%fused_computation.13 | loop fusion | flops 6518752 | bytes 9719936 | tf_op jit(solution)/shard_map/transpose(jvp())/add_any | solution.py:27
  148.6 2.4 %collective-permute-start.11 = (f32[8,1,1040]{2,1,0:T(1,128)}, f32[8,1,1040]{2,1,0:T(1,128)}, u32[]{:S(2)}, u32[]{:S(2)}) collective-permute-start(f32[8,1,1040]{2,1,0:T(1,128)} %get-tuple-element.51), channel_id=1, source_target_pairs={{0,8},{8,16},{16,24},{24,32},{32,40},{40,48},{48,56},{56,64},{64,7... | collective-permute-start | bytes 99848 | tf_op jit(solution)/shard_map/transpose(jvp())/ppermute | solution.py:20
  152.4 4.4 %all-to-all-start.2 = ((f32[8,32,1024]{2,1,0:T(8,128)}), f32[8,32,1024]{2,1,0:T(8,128)}, u32[]{:S(2)}, u32[]{:S(2)}) async-start(f32[8,32,1024]{2,1,0:T(8,128)} %slice.509), calls=%async_computation.2 | async-start | bytes 2097152 | tf_op jit(solution)/shard_map/all_to_all | solution.py:102
  156.8 2.0 collective-permute-done.11
  162.1 4.6 %multiply_add_fusion = f32[8,34,1042]{2,1,0:T(8,128)S(1)} fusion(f32[8,32,1040]{2,1,0:T(8,128)S(1)} %get-tuple-element.7, f32[8,32,1040]{2,1,0:T(8,128)S(1)} %get-tuple-element.6, f32[8,32,1040]{2,1,0:T(8,128)S(1)} %get-tuple-element.39, f32[8,32,1040]{2,1,0:T(8,128)S(1)} %get-tuple-element.40, f32[8,32,1040]{2,1,0:T(8,128)S(1)} %get-tuple-element.41, ...), kind=kLoop, calls=%fused_computation.12 | loop fusion | flops 6518752 | bytes 9719936 | tf_op jit(solution)/shard_map/transpose(jvp())/add_any | solution.py:27
  166.9 5.4 %collective-permute-start.12 = (f32[8,1,1040]{2,1,0:T(1,128)S(1)}, f32[8,1,1040]{2,1,0:T(1,128)S(1)}, u32[]{:S(2)}, u32[]{:S(2)}) collective-permute-start(f32[8,1,1040]{2,1,0:T(1,128)S(1)} %get-tuple-element.48), channel_id=1, source_target_pairs={{8,0},{16,8},{24,16},{32,24},{40,32},{48,40},{56,48},{64,56},{72,6... | collective-permute-start | bytes 99848 | tf_op jit(solution)/shard_map/transpose(jvp())/ppermute | solution.py:18
  172.3 1.9 collective-permute-start.13
  174.3 7.7 %collective-permute-done.13 = f32[8,1,1040]{2,1,0:T(1,128)S(1)} collective-permute-done((f32[8,1,1040]{2,1,0:T(1,128)S(1)}, f32[8,1,1040]{2,1,0:T(1,128)S(1)}, u32[]{:S(2)}, u32[]{:S(2)}) %collective-permute-start.13) | collective-permute-done | bytes 33312 | tf_op jit(solution)/shard_map/transpose(jvp())/ppermute | solution.py:20
  182.1 2.3 %multiply_reduce_fusion.2 = (f32[32,1040]{1,0:T(8,128)S(1)}, f32[32,1040]{1,0:T(8,128)S(1)}, f32[32,1040]{1,0:T(8,128)S(1)}, f32[32,1040]{1,0:T(8,128)S(1)}) fusion(f32[8,32,1040]{2,1,0:T(8,128)S(1)} %copy-done.18, f32[8,32,1040]{2,1,0:T(8,128)S(1)} %copy-done.12, pred[1040]{0:T(1024)(128)(4,1)S(1)} %fusion.117, f32[8,32,1040]{2,1,0:T(8,128)S(1)} %copy-done.17, ...), kind=kLoop, calls=%fused_computation.129 | loop fusion | flops 5724160 | bytes 9252880 | tf_op jit(solution)/shard_map/transpose(jvp())/reduce_sum | solution.py:47
  185.7 5.6 %all-to-all-start.4 = ((f32[8,32,1024]{2,1,0:T(8,128)}), f32[8,32,1024]{2,1,0:T(8,128)S(1)}, u32[]{:S(2)}, u32[]{:S(2)}) async-start(f32[8,32,1024]{2,1,0:T(8,128)} %stack.166), calls=%async_computation.4 | async-start | bytes 2097152 | tf_op jit(solution)/shard_map/all_to_all | solution.py:104
  191.4 2.3 %copy.12 = f32[1,8,4,8,1024]{4,3,1,2,0:T(8,128)} copy(f32[1,8,4,8,1024]{4,3,2,1,0:T(8,128)} %bitcast.59) | data formatting | bytes 2097152 | tf_op jit(solution)/shard_map/all_to_all | solution.py:102
  193.7 7.7 %all-to-all-done.4 = f32[8,32,1024]{2,1,0:T(8,128)S(1)} async-done(((f32[8,32,1024]{2,1,0:T(8,128)}), f32[8,32,1024]{2,1,0:T(8,128)S(1)}, u32[]{:S(2)}, u32[]{:S(2)}) %all-to-all-start.4) | async-done | bytes 1048608 | tf_op jit(solution)/shard_map/all_to_all | solution.py:104
  (153 shorter events, 48.7 us)
Async XLA Ops:
  7.8 21.7 %all-to-all-start.1 = ((f32[8,32,1040]{2,1,0:T(8,128)}), f32[8,32,1040]{2,1,0:T(8,128)S(1)}, u32[]{:S(2)}, u32[]{:S(2)}) async-start(f32[8,32,1040]{2,1,0:T(8,128)} %fusion.80), calls=%async_computation.1 | async-start | bytes 2359296 | tf_op jit(solution)/shard_map/all_to_all | solution.py:77
  21.0 118.4 %copy-start.19 = (f32[32,1040]{1,0:T(8,128)}, f32[32,1040]{1,0:T(8,128)S(1)}, u32[]{:S(2)}) copy-start(f32[32,1040]{1,0:T(8,128)S(1)} %get-tuple-element.12) | copy-start | bytes 399364
  29.5 18.4 %copy-start.6 = (f32[8,32,1040]{2,1,0:T(8,128)}, f32[8,32,1040]{2,1,0:T(8,128)S(1)}, u32[]{:S(2)}) copy-start(f32[8,32,1040]{2,1,0:T(8,128)S(1)} %all-to-all-done.1) | copy-start | bytes 3194884
  29.5 65.8 %all-to-all-start = ((f32[8,32,1040]{2,1,0:T(8,128)}), f32[8,32,1040]{2,1,0:T(8,128)S(1)}, u32[]{:S(2)}, u32[]{:S(2)}) async-start(f32[8,32,1040]{2,1,0:T(8,128)} %fusion.76), calls=%async_computation | async-start | bytes 2359296 | tf_op jit(solution)/shard_map/all_to_all | solution.py:77
  33.7 9.8 %collective-permute-start = (f32[8,1,1040]{2,1,0:T(1,128)S(1)}, f32[8,1,1040]{2,1,0:T(1,128)S(1)}, u32[]{:S(2)}, u32[]{:S(2)}) collective-permute-start(f32[8,1,1040]{2,1,0:T(1,128)S(1)} %get-tuple-element.75), channel_id=1, source_target_pairs={{0,8},{8,16},{16,24},{24,32},{32,40},{40,48},{48,56},{56,64},{64,7... | collective-permute-start | bytes 99848 | tf_op jit(solution)/shard_map/jvp()/ppermute | solution.py:18
  35.6 11.6 %collective-permute-start.1 = (f32[8,1,1040]{2,1,0:T(1,128)S(1)}, f32[8,1,1040]{2,1,0:T(1,128)S(1)}, u32[]{:S(2)}, u32[]{:S(2)}) collective-permute-start(f32[8,1,1040]{2,1,0:T(1,128)S(1)} %get-tuple-element.76), channel_id=1, source_target_pairs={{8,0},{16,8},{24,16},{32,24},{40,32},{48,40},{56,48},{64,56},{72,6... | collective-permute-start | bytes 99848 | tf_op jit(solution)/shard_map/jvp()/ppermute | solution.py:20
  47.9 13.0 %copy-start.10 = (f32[1,32,8192]{2,1,0:T(8,128)S(1)}, f32[1,32,8192]{2,1,0:T(8,128)}, u32[]{:S(2)}) copy-start(f32[1,32,8192]{2,1,0:T(8,128)} %param.11) | copy-start | bytes 3145732
  50.9 12.3 %copy-start = (f32[8,32,1040]{2,1,0:T(8,128)}, f32[8,32,1040]{2,1,0:T(8,128)S(1)}, u32[]{:S(2)}) copy-start(f32[8,32,1040]{2,1,0:T(8,128)S(1)} %get-tuple-element.32) | copy-start | bytes 3194884
  51.0 10.7 %collective-permute-start.2 = (f32[8,1,1040]{2,1,0:T(1,128)S(1)}, f32[8,1,1040]{2,1,0:T(1,128)S(1)}, u32[]{:S(2)}, u32[]{:S(2)}) collective-permute-start(f32[8,1,1040]{2,1,0:T(1,128)S(1)} %get-tuple-element.73), channel_id=1, source_target_pairs={{0,8},{8,16},{16,24},{24,32},{32,40},{40,48},{48,56},{56,64},{64,7... | collective-permute-start | bytes 99848 | tf_op jit(solution)/shard_map/jvp()/ppermute | solution.py:18
  52.9 9.7 %collective-permute-start.3 = (f32[8,1,1040]{2,1,0:T(1,128)S(1)}, f32[8,1,1040]{2,1,0:T(1,128)S(1)}, u32[]{:S(2)}, u32[]{:S(2)}) collective-permute-start(f32[8,1,1040]{2,1,0:T(1,128)S(1)} %get-tuple-element.74), channel_id=1, source_target_pairs={{8,0},{16,8},{24,16},{32,24},{40,32},{48,40},{56,48},{64,56},{72,6... | collective-permute-start | bytes 99848 | tf_op jit(solution)/shard_map/jvp()/ppermute | solution.py:20
  66.2 12.2 %copy-start.2 = (f32[8,32,1040]{2,1,0:T(8,128)}, f32[8,32,1040]{2,1,0:T(8,128)S(1)}, u32[]{:S(2)}) copy-start(f32[8,32,1040]{2,1,0:T(8,128)S(1)} %get-tuple-element.30) | copy-start | bytes 3194884
  66.3 10.6 %collective-permute-start.4 = (f32[8,1,1040]{2,1,0:T(1,128)S(1)}, f32[8,1,1040]{2,1,0:T(1,128)S(1)}, u32[]{:S(2)}, u32[]{:S(2)}) collective-permute-start(f32[8,1,1040]{2,1,0:T(1,128)S(1)} %get-tuple-element.71), channel_id=1, source_target_pairs={{0,8},{8,16},{16,24},{24,32},{32,40},{40,48},{48,56},{56,64},{64,7... | collective-permute-start | bytes 99848 | tf_op jit(solution)/shard_map/jvp()/ppermute | solution.py:18
  68.2 9.5 %collective-permute-start.5 = (f32[8,1,1040]{2,1,0:T(1,128)S(1)}, f32[8,1,1040]{2,1,0:T(1,128)S(1)}, u32[]{:S(2)}, u32[]{:S(2)}) collective-permute-start(f32[8,1,1040]{2,1,0:T(1,128)S(1)} %get-tuple-element.72), channel_id=1, source_target_pairs={{8,0},{16,8},{24,16},{32,24},{40,32},{48,40},{56,48},{64,56},{72,6... | collective-permute-start | bytes 99848 | tf_op jit(solution)/shard_map/jvp()/ppermute | solution.py:20
  81.4 11.5 %copy-start.4 = (f32[8,32,1040]{2,1,0:T(8,128)}, f32[8,32,1040]{2,1,0:T(8,128)S(1)}, u32[]{:S(2)}) copy-start(f32[8,32,1040]{2,1,0:T(8,128)S(1)} %get-tuple-element.28) | copy-start | bytes 3194884
  81.5 10.6 %collective-permute-start.6 = (f32[8,1,1040]{2,1,0:T(1,128)S(1)}, f32[8,1,1040]{2,1,0:T(1,128)S(1)}, u32[]{:S(2)}, u32[]{:S(2)}) collective-permute-start(f32[8,1,1040]{2,1,0:T(1,128)S(1)} %get-tuple-element.69), channel_id=1, source_target_pairs={{0,8},{8,16},{16,24},{24,32},{32,40},{40,48},{48,56},{56,64},{64,7... | collective-permute-start | bytes 99848 | tf_op jit(solution)/shard_map/jvp()/ppermute | solution.py:18
  83.4 9.5 %collective-permute-start.7 = (f32[8,1,1040]{2,1,0:T(1,128)S(1)}, f32[8,1,1040]{2,1,0:T(1,128)S(1)}, u32[]{:S(2)}, u32[]{:S(2)}) collective-permute-start(f32[8,1,1040]{2,1,0:T(1,128)S(1)} %get-tuple-element.70), channel_id=1, source_target_pairs={{8,0},{16,8},{24,16},{32,24},{40,32},{48,40},{56,48},{64,56},{72,6... | collective-permute-start | bytes 99848 | tf_op jit(solution)/shard_map/jvp()/ppermute | solution.py:20
  95.3 17.8 %all-to-all-start.3 = ((f32[8,32,1040]{2,1,0:T(8,128)}), f32[8,32,1040]{2,1,0:T(8,128)}, u32[]{:S(2)}, u32[]{:S(2)}) async-start(f32[8,32,1040]{2,1,0:T(8,128)} %fusion.84), calls=%async_computation.3 | async-start | bytes 2359296 | tf_op jit(solution)/shard_map/all_to_all | solution.py:77
  121.4 10.0 %collective-permute-start.8 = (f32[8,1,1040]{2,1,0:T(1,128)S(1)}, f32[8,1,1040]{2,1,0:T(1,128)S(1)}, u32[]{:S(2)}, u32[]{:S(2)}) collective-permute-start(f32[8,1,1040]{2,1,0:T(1,128)S(1)} %get-tuple-element.52), channel_id=1, source_target_pairs={{8,0},{16,8},{24,16},{32,24},{40,32},{48,40},{56,48},{64,56},{72,6... | collective-permute-start | bytes 99848 | tf_op jit(solution)/shard_map/transpose(jvp())/ppermute | solution.py:18
  129.5 9.9 %collective-permute-start.9 = (f32[8,1,1040]{2,1,0:T(1,128)S(1)}, f32[8,1,1040]{2,1,0:T(1,128)S(1)}, u32[]{:S(2)}, u32[]{:S(2)}) collective-permute-start(f32[8,1,1040]{2,1,0:T(1,128)S(1)} %get-tuple-element.53), channel_id=1, source_target_pairs={{0,8},{8,16},{16,24},{24,32},{32,40},{40,48},{48,56},{56,64},{64,7... | collective-permute-start | bytes 99848 | tf_op jit(solution)/shard_map/transpose(jvp())/ppermute | solution.py:20
  146.7 10.1 %collective-permute-start.10 = (f32[8,1,1040]{2,1,0:T(1,128)}, f32[8,1,1040]{2,1,0:T(1,128)}, u32[]{:S(2)}, u32[]{:S(2)}) collective-permute-start(f32[8,1,1040]{2,1,0:T(1,128)} %get-tuple-element.50), channel_id=1, source_target_pairs={{8,0},{16,8},{24,16},{32,24},{40,32},{48,40},{56,48},{64,56},{72,6... | collective-permute-start | bytes 99848 | tf_op jit(solution)/shard_map/transpose(jvp())/ppermute | solution.py:18
  148.6 10.1 %collective-permute-start.11 = (f32[8,1,1040]{2,1,0:T(1,128)}, f32[8,1,1040]{2,1,0:T(1,128)}, u32[]{:S(2)}, u32[]{:S(2)}) collective-permute-start(f32[8,1,1040]{2,1,0:T(1,128)} %get-tuple-element.51), channel_id=1, source_target_pairs={{0,8},{8,16},{16,24},{24,32},{32,40},{40,48},{48,56},{56,64},{64,7... | collective-permute-start | bytes 99848 | tf_op jit(solution)/shard_map/transpose(jvp())/ppermute | solution.py:20
  152.4 32.3 %all-to-all-start.2 = ((f32[8,32,1024]{2,1,0:T(8,128)}), f32[8,32,1024]{2,1,0:T(8,128)}, u32[]{:S(2)}, u32[]{:S(2)}) async-start(f32[8,32,1024]{2,1,0:T(8,128)} %slice.509), calls=%async_computation.2 | async-start | bytes 2097152 | tf_op jit(solution)/shard_map/all_to_all | solution.py:102
  162.0 20.0 %copy-start.12 = (f32[8,32,1040]{2,1,0:T(8,128)S(1)}, f32[8,32,1040]{2,1,0:T(8,128)}, u32[]{:S(2)}) copy-start(f32[8,32,1040]{2,1,0:T(8,128)} %copy-done.11) | copy-start | bytes 3194884
  162.0 20.0 %copy-start.15 = (f32[8,32,1040]{2,1,0:T(8,128)S(1)}, f32[8,32,1040]{2,1,0:T(8,128)}, u32[]{:S(2)}) copy-start(f32[8,32,1040]{2,1,0:T(8,128)} %get-tuple-element.33) | copy-start | bytes 3194884
  162.0 20.0 %copy-start.16 = (f32[8,32,1040]{2,1,0:T(8,128)S(1)}, f32[8,32,1040]{2,1,0:T(8,128)}, u32[]{:S(2)}) copy-start(f32[8,32,1040]{2,1,0:T(8,128)} %get-tuple-element.31) | copy-start | bytes 3194884
  162.0 20.0 %copy-start.17 = (f32[8,32,1040]{2,1,0:T(8,128)S(1)}, f32[8,32,1040]{2,1,0:T(8,128)}, u32[]{:S(2)}) copy-start(f32[8,32,1040]{2,1,0:T(8,128)} %get-tuple-element.29) | copy-start | bytes 3194884
  162.1 20.0 %copy-start.18 = (f32[8,32,1040]{2,1,0:T(8,128)S(1)}, f32[8,32,1040]{2,1,0:T(8,128)}, u32[]{:S(2)}) copy-start(f32[8,32,1040]{2,1,0:T(8,128)} %get-tuple-element.27) | copy-start | bytes 3194884
  162.1 20.0 %copy-start.22 = (f32[8,1,1040]{2,1,0:T(1,128)S(1)}, f32[8,1,1040]{2,1,0:T(1,128)}, u32[]{:S(2)}) copy-start(f32[8,1,1040]{2,1,0:T(1,128)} %copy-done.21) | copy-start | bytes 99844
  162.1 20.0 %copy-start.24 = (f32[8,1,1040]{2,1,0:T(1,128)S(1)}, f32[8,1,1040]{2,1,0:T(1,128)}, u32[]{:S(2)}) copy-start(f32[8,1,1040]{2,1,0:T(1,128)} %copy-done.23) | copy-start | bytes 99844
  166.9 7.4 %collective-permute-start.12 = (f32[8,1,1040]{2,1,0:T(1,128)S(1)}, f32[8,1,1040]{2,1,0:T(1,128)S(1)}, u32[]{:S(2)}, u32[]{:S(2)}) collective-permute-start(f32[8,1,1040]{2,1,0:T(1,128)S(1)} %get-tuple-element.48), channel_id=1, source_target_pairs={{8,0},{16,8},{24,16},{32,24},{40,32},{48,40},{56,48},{64,56},{72,6... | collective-permute-start | bytes 99848 | tf_op jit(solution)/shard_map/transpose(jvp())/ppermute | solution.py:18
  172.3 9.7 %collective-permute-start.13 = (f32[8,1,1040]{2,1,0:T(1,128)S(1)}, f32[8,1,1040]{2,1,0:T(1,128)S(1)}, u32[]{:S(2)}, u32[]{:S(2)}) collective-permute-start(f32[8,1,1040]{2,1,0:T(1,128)S(1)} %get-tuple-element.49), channel_id=1, source_target_pairs={{0,8},{8,16},{16,24},{24,32},{32,40},{40,48},{48,56},{56,64},{64,7... | collective-permute-start | bytes 99848 | tf_op jit(solution)/shard_map/transpose(jvp())/ppermute | solution.py:20
  185.7 15.7 %all-to-all-start.4 = ((f32[8,32,1024]{2,1,0:T(8,128)}), f32[8,32,1024]{2,1,0:T(8,128)S(1)}, u32[]{:S(2)}, u32[]{:S(2)}) async-start(f32[8,32,1024]{2,1,0:T(8,128)} %stack.166), calls=%async_computation.4 | async-start | bytes 2097152 | tf_op jit(solution)/shard_map/all_to_all | solution.py:104
  (24 other events, 61.5 us)
